TPU v7x, 32 devices: a whole 2x2x4 slice. The times are simulated.
32 devices in a mesh: rows: 8 (over y, x, core), rhs: 4 (over z).
Axes of the slice: x: 2, y: 2, z: 4, core: 2. Of those that a mesh axis runs over, the one named last changes fastest.
Arguments:
- samples: float32 [65536, 16], P(('rows', 'rhs')), may hold values from -5 to 5
- freq_table: float32 [4096, 16], replicated, may hold values from -3 to 3
- feature_seeds: int32 [512], replicated, may hold values from 0 to 4095
- phases: float32 [512], replicated, may hold values from -3.140625 to 3.140625
- treatment_features: bfloat16 [65536, 512], P('rows', 'rhs'), may hold values from -2.5 to 2.5, as said below
Outputs:
- coefficients: float32 [512, 512], replicated
- fitted: float32 [65536, 512], P(('rows', 'rhs'))
Inputs may be any that keep to these rules, and one draw needn't show every extreme that they name: `treatment_features`: treatment features depend on the instrument values.
All inputs are finite; a program needn't handle non-finite values.
Results may differ from a plain program's by a relative error of at most 0.0008.
The roundings to bfloat16 on the way count: a program that leaves them out, or rounds other values in their place, can miss the bound.
Values may be sent and summed in bfloat16 or wider, within the bound.
A program may use at most 64 MiB of HBM per device.

v0:
```python
import jax
import jax.numpy as jnp
from jax import lax
from jax.sharding import PartitionSpec as P

ridge = 0.05


def solve_with(factor, right):
    lower = lax.linalg.triangular_solve(factor, right, left_side=True, lower=True)
    return lax.linalg.triangular_solve(factor, lower, left_side=True, lower=True, transpose_a=True)


def features_of(values, freqs, phases):
    angles = (
        jnp.dot(
            values, freqs.T, precision=lax.Precision.HIGHEST, preferred_element_type=jnp.float32
        )
        + phases
    )
    return (jnp.sqrt(jnp.float32(2.0)) * jnp.cos(angles)).astype(jnp.bfloat16)


def body(samples, freq_table, feature_seeds, phases, treatment_features):
    own_rows = samples.shape[0]
    count = own_rows * lax.axis_size("rows") * lax.axis_size("rhs")
    freqs = freq_table[feature_seeds]
    contract = (((0,), (0,)), ((), ()))
    instruments = features_of(samples, freqs, phases)
    gram_part = lax.dot_general(
        instruments, instruments, contract, preferred_element_type=jnp.float32
    )
    gram = lax.psum(gram_part, ("rows", "rhs")) / count
    gram = gram + ridge * jnp.eye(gram.shape[0], dtype=jnp.float32)
    factor = jnp.linalg.cholesky(gram)
    targets = lax.all_to_all(treatment_features, "rhs", split_axis=0, concat_axis=1, tiled=True)
    cross_part = lax.dot_general(instruments, targets, contract, preferred_element_type=jnp.float32)
    cross = lax.psum(cross_part, ("rows", "rhs")) / count
    coefficients = solve_with(factor, cross)
    fitted = jnp.dot(
        instruments, coefficients.astype(jnp.bfloat16), preferred_element_type=jnp.float32
    )
    return (coefficients, fitted)


def solution(mesh):
    placed = (P(("rows", "rhs"), None), P(), P(), P(), P("rows", "rhs"))
    return jax.shard_map(
        body, mesh=mesh, in_specs=placed, out_specs=(P(), P(("rows", "rhs"), None)), check_vma=False
    )
```

profile of v0, /device:TPU:0, one launch (start us, length us, event | category | flops | bytes accessed | tf_op | source)
XLA Modules:
  0.0 364.7 jit_solution(18324534306063840201)
XLA Ops:
  7.2 6.5 %all-to-all-start = ((bf16[4,2048,128]{2,1,0:T(8,128)(2,1)}), bf16[4,2048,128]{2,1,0:T(8,128)(2,1)S(1)}, u32[]{:S(2)}, u32[]{:S(2)}) async-start(bf16[4,2048,128]{2,1,0:T(8,128)(2,1)} %bitcast.66), calls=%async_computation | async-start | bytes 4194304 | tf_op jit(solution)/shard_map/all_to_all | solution.py:36
  13.7 1.9 copy.31
  15.7 2.6 gather_fusion
  18.3 17.9 %multiply_convert_fusion = bf16[512,2048]{1,0:T(8,128)(2,1)S(1)} fusion(f32[512,16]{1,0:T(8,128)S(1)} %gather_fusion, f32[2048,16]{0,1:T(8,128)S(1)} %copy-done, f32[512]{0:T(512)S(1)} %copy-done.8), kind=kOutput, calls=%fused_computation.3 | convolution fusion | flops 204472320 | bytes 2263040 | tf_op jit(solution)/shard_map/dot_general | solution.py:16
  37.6 2.3 fusion.50
  39.8 22.0 %all-to-all-done = bf16[4,2048,128]{2,1,0:T(8,128)(2,1)S(1)} async-done(((bf16[4,2048,128]{2,1,0:T(8,128)(2,1)}), bf16[4,2048,128]{2,1,0:T(8,128)(2,1)S(1)}, u32[]{:S(2)}, u32[]{:S(2)}) %all-to-all-start) | async-done | bytes 2097184 | tf_op jit(solution)/shard_map/all_to_all | solution.py:36
  61.9 2.8 copy.42
  64.7 4.5 %fusion.51 = f32[512,512]{0,1:T(8,128)} fusion(bf16[512,2048]{1,0:T(8,128)(2,1)} %copy-done.3, bf16[2048,512]{0,1:T(8,128)(2,1)} %bitcast.67), kind=kOutput, calls=%fused_computation.97 | convolution fusion | flops 1073741824 | bytes 5242880 | tf_op jit(solution)/shard_map/dot_general | solution.py:37
  69.2 133.9 %all-reduce.4.cloned.1.call-done = (f32[512,512]{0,1:T(8,128)}, f32[512,512]{0,1:T(8,128)}) async-done(((f32[512,512]{0,1:T(8,128)}, f32[512,512]{0,1:T(8,128)}), (f32[512,512]{0,1:T(8,128)}, f32[512,512]{0,1:T(8,128)})) %all-reduce.4.cloned.1.call-update) | async-done | bytes 2097168 | tf_op jit(solution)/shard_map/psum | solution.py:38
  203.1 2.8 select_add_fusion
  205.9 1.6 copy.33
  208.8 11.7 %cholesky.103 = f32[128,128]{1,0:T(8,128)S(1)} custom-call(f32[128,128]{1,0:T(8,128)S(1)} %cholesky.263), custom_call_target="Cholesky" | custom-call | tf_op jit(solution)/shard_map/jit(cholesky)/cholesky | solution.py:35
  220.6 9.8 %custom-call.32 = f32[1,128,128]{1,2,0:T(8,128)S(1)} custom-call(f32[1,128,128]{2,1,0:T(8,128)S(1)} %get-tuple-element.39), custom_call_target="InvertDiagBlocksLowerTriangular" | custom-call | tf_op jit(solution)/shard_map/jit(cholesky)/cholesky | solution.py:35
  233.1 12.1 %cholesky.215 = f32[128,128]{1,0:T(8,128)S(1)} custom-call(f32[128,128]{1,0:T(8,128)S(1)} %cholesky.267), custom_call_target="Cholesky" | custom-call | tf_op jit(solution)/shard_map/jit(cholesky)/cholesky | solution.py:35
  245.3 9.8 %custom-call.33 = f32[1,128,128]{1,2,0:T(8,128)S(1)} custom-call(f32[1,128,128]{2,1,0:T(8,128)S(1)} %get-tuple-element.37), custom_call_target="InvertDiagBlocksLowerTriangular" | custom-call | tf_op jit(solution)/shard_map/jit(cholesky)/cholesky | solution.py:35
  255.6 1.5 convolution_subtract_fusion.7
  257.1 11.7 %cholesky.236 = f32[128,128]{1,0:T(8,128)S(1)} custom-call(f32[128,128]{1,0:T(8,128)S(1)} %cholesky.272), custom_call_target="Cholesky" | custom-call | tf_op jit(solution)/shard_map/jit(cholesky)/cholesky | solution.py:35
  269.0 9.8 %custom-call.34 = f32[1,128,128]{1,2,0:T(8,128)S(1)} custom-call(f32[1,128,128]{2,1,0:T(8,128)S(1)} %get-tuple-element.35), custom_call_target="InvertDiagBlocksLowerTriangular" | custom-call | tf_op jit(solution)/shard_map/jit(cholesky)/cholesky | solution.py:35
  280.4 11.9 %cholesky.253 = f32[128,128]{1,0:T(8,128)S(1)} custom-call(f32[128,128]{1,0:T(8,128)S(1)} %convolution_subtract_fusion.8), custom_call_target="Cholesky" | custom-call | tf_op jit(solution)/shard_map/jit(cholesky)/cholesky | solution.py:35
  297.8 8.9 %while.1 = (s32[]{:T(128)}, f32[512,512]{0,1:T(8,128)S(1)}, s32[4,2]{0,1:T(2,128)S(1)}, f32[4,128,128]{2,1,0:T(8,128)S(1)}, s32[]{:T(128)}) while((s32[]{:T(128)}, f32[512,512]{0,1:T(8,128)S(1)}, s32[4,2]{0,1:T(2,128)S(1)}, f32[4,128,128]{2,1,0:T(8,128)S(1)}, s32[]{:T(128)}) %tuple.30), condition=%wide.while_cond, body=%wide.while_body.sunk | while | flops 2 | bytes 393329 | solution.py:11
  298.5 1.4 dynamic-slice.7
  306.7 39.3 %custom-call.35 = f32[4,128,128]{1,2,0:T(8,128)S(1)} custom-call(f32[4,128,128]{2,1,0:T(8,128)S(1)} %get-tuple-element.9), custom_call_target="InvertDiagBlocksLowerTriangular" | custom-call | tf_op jit(solution)/shard_map/triangular_solve | solution.py:11
  348.9 1.5 convolution_subtract_fusion.5
  354.3 3.3 fusion.17
  (86 shorter events, 24.7 us)
Async XLA Ops:
  7.2 11.2 %copy-start = (f32[2048,16]{0,1:T(8,128)S(1)}, f32[2048,16]{0,1:T(8,128)}, u32[]{:S(2)}) copy-start(f32[2048,16]{0,1:T(8,128)} %param.5) | copy-start | bytes 393220
  7.2 6.6 %copy-start.6 = (f32[4096,16]{0,1:T(8,128)S(1)}, f32[4096,16]{0,1:T(8,128)}, u32[]{:S(2)}) copy-start(f32[4096,16]{0,1:T(8,128)} %param.6) | copy-start | bytes 786436
  7.2 54.7 %all-to-all-start = ((bf16[4,2048,128]{2,1,0:T(8,128)(2,1)}), bf16[4,2048,128]{2,1,0:T(8,128)(2,1)S(1)}, u32[]{:S(2)}, u32[]{:S(2)}) async-start(bf16[4,2048,128]{2,1,0:T(8,128)(2,1)} %bitcast.66), calls=%async_computation | async-start | bytes 4194304 | tf_op jit(solution)/shard_map/all_to_all | solution.py:36
  13.7 2.0 copy-start.7
  13.7 4.6 %copy-start.8 = (f32[512]{0:T(512)S(1)}, f32[512]{0:T(512)}, u32[]{:S(2)}) copy-start(f32[512]{0:T(512)} %param.8) | copy-start | bytes 6148
  13.7 189.4 %all-reduce.4.cloned.1.call-start = ((), (), s32[]{:S(2)}) async-start(), calls=%async_computation.1 | async-start | bytes 4194304 | tf_op jit(solution)/shard_map/psum | solution.py:38
  36.2 1.3 copy-start.3
  205.9 1.7 copy-start.2
  207.8 1.0 copy-start.5
  352.7 1.6 copy-start.4
  354.3 3.3 copy-start.1
Sparse Core Ops, SparseCore 0:
  69.3 133.7 all-reduce.3
where the time goes:
time: 369 us; the launch traced here: 365 us
  waiting for transfers between devices  156 us (42%)
  other arithmetic  122 us (33%)
  matrix products  41.5 us (11%)
  local copies, waits for them, and re-layouts  21.3 us (6%)
  between operations  17.2 us (5%)
  starting transfers between devices  6.53 us (2%)
    psum x1, waiting for transfers between devices, body(): cross = lax.psum(cross_part, ('rows', 'rhs')) / count  134 us
    another operation x15, other arithmetic, body(): factor = jnp.linalg.cholesky(gram)  79.6 us
    another operation x4, other arithmetic, solve_with(): lax.linalg.triangular_solve(factor, lower, left_side=True, lower=True, tr...  39.5 us
    all_to_all x1, waiting for transfers between devices, body(): lax.all_to_all(treatment_features, 'rhs', split_axis=0, concat_axis=1, ti...  22 us
    dot_general x1, matrix products, features_of(): jnp.dot(values, freqs.T, precision=lax.Precision.HIGHEST, preferred_eleme...  17.9 us
    another operation x20, local copies, waits for them, and re-layouts  8.79 us
  transfers between devices with their start and end apart: 2, of which 2 were waited for; matrix products, arithmetic and copies ran while one was open for 7% of the time, Pallas kernels for 0%

commit v1 on v0

v1 whole, which is shorter than its diff:
```python
import functools
import math

import jax
import jax.numpy as jnp
from jax import lax
from jax.experimental import pallas as pl
from jax.experimental.pallas import tpu as pltpu
from jax.sharding import PartitionSpec as P

ridge = 0.05
MESH = pl.DeviceIdType.MESH
HIGHEST = lax.Precision.HIGHEST
VMEM = pl.BlockSpec(memory_space=pltpu.VMEM)
NT = (((1,), (1,)), ((), ()))
TILE = 128
SIN_TERMS = [
    (-1.0) ** k * math.pi ** (2 * k + 1) / math.factorial(2 * k + 1) for k in range(7)
]


def split_low(x):
    high = lax.reduce_precision(x, 8, 7)
    rest = x - high
    middle = lax.reduce_precision(rest, 8, 7)
    low = rest - middle
    return tuple(t.astype(jnp.bfloat16) for t in (high, middle, low))


def gather_kernel(group, x_ref, out_ref, send, recv):
    me = lax.axis_index("rhs")
    barrier = pltpu.get_barrier_semaphore()
    for d in range(1, group):
        pl.semaphore_signal(
            barrier, inc=1, device_id={"rhs": lax.rem(me + d, group)}, device_id_type=MESH
        )
    pl.semaphore_wait(barrier, group - 1)
    copies = []
    for d in range(1, group):
        copy = pltpu.make_async_remote_copy(
            src_ref=x_ref,
            dst_ref=out_ref.at[me],
            send_sem=send.at[d],
            recv_sem=recv.at[d],
            device_id={"rhs": lax.rem(me + d, group)},
            device_id_type=MESH,
        )
        copy.start()
        copies.append(copy)
    out_ref[me] = x_ref[...]
    for copy in copies:
        copy.wait()


def gather_samples(x):
    group = lax.axis_size("rhs")
    return pl.pallas_call(
        functools.partial(gather_kernel, group),
        out_shape=jax.ShapeDtypeStruct((group,) + x.shape, x.dtype),
        in_specs=[VMEM],
        out_specs=VMEM,
        scratch_shapes=[pltpu.SemaphoreType.DMA((group,))] * 2,
        compiler_params=pltpu.CompilerParams(collective_id=0, has_side_effects=True),
    )(x)


def panel_kernel(me_ref, x_ref, f_ref, t_ref, acc_ref, own_ref, phi_ref):
    block, part = pl.program_id(0), pl.program_id(1)
    me = me_ref[0]
    panel = t_ref.shape[1]
    chunk = t_ref.shape[0]
    x = x_ref[0]
    high = x.astype(jnp.bfloat16)
    rest = x - high.astype(jnp.float32)
    middle = rest.astype(jnp.bfloat16)
    low = (rest - middle.astype(jnp.float32)).astype(jnp.bfloat16)
    ones = jnp.ones(x.shape, jnp.bfloat16)
    rows = jnp.concatenate([high, high, middle, middle, high, low, ones], axis=0)
    turns = jnp.dot(f_ref[...], rows, preferred_element_type=jnp.float32)
    r = turns - jnp.round(turns)
    u = r * r
    scale = math.sqrt(2.0 * math.sqrt(2.0))
    s = jnp.full_like(u, SIN_TERMS[-1] * scale)
    for term in reversed(SIN_TERMS[:-1]):
        s = s * u + term * scale
    s = s * r
    phi = (math.sqrt(2.0) - s * s).astype(jnp.bfloat16)
    phi_ref[...] = phi

    @pl.when(jnp.logical_and(block == 0, part == 0))
    def _():
        acc_ref[...] = jnp.zeros_like(acc_ref)

    mine = phi_ref[pl.ds(pl.multiple_of(me * panel, panel), panel), :]
    acc_ref[:, :panel] += lax.dot_general(
        phi, mine, NT, preferred_element_type=jnp.float32
    )
    acc_ref[:, panel:] += jnp.dot(phi, t_ref[...], preferred_element_type=jnp.float32)

    @pl.when(block == me)
    def _():
        own_ref[part] = phi


def panels(me, gathered, freqs, targets):
    group, depth, own = gathered.shape
    features = freqs.shape[0]
    panel = targets.shape[1]
    chunk = min(own, 1024)
    parts = own // chunk
    return pl.pallas_call(
        panel_kernel,
        grid_spec=pltpu.PrefetchScalarGridSpec(
            num_scalar_prefetch=1,
            grid=(group, parts),
            in_specs=[
                pl.BlockSpec((1, depth, chunk), lambda i, j, me: (i, 0, j)),
                pl.BlockSpec(freqs.shape, lambda i, j, me: (0, 0)),
                pl.BlockSpec((chunk, panel), lambda i, j, me: (i * parts + j, 0)),
            ],
            out_specs=[
                pl.BlockSpec((features, 2 * panel), lambda i, j, me: (0, 0)),
                pl.BlockSpec((parts, features, chunk), lambda i, j, me: (0, 0, 0)),
            ],
            scratch_shapes=[pltpu.VMEM((features, chunk), jnp.bfloat16)],
        ),
        out_shape=[
            jax.ShapeDtypeStruct((features, 2 * panel), jnp.float32),
            jax.ShapeDtypeStruct((parts, features, chunk), jnp.bfloat16),
        ],
    )(me, gathered, freqs, targets)


def reduce_kernel(R, Z, w_ref, out_ref, got, send, recv, zsend, zrecv, psend, precv, csend, crecv):
    r, z = lax.axis_index("rows"), lax.axis_index("rhs")
    core = lax.rem(r, 2)
    sibling = r + 1 - 2 * core
    barrier = pltpu.get_barrier_semaphore()
    for d in range(1, R):
        pl.semaphore_signal(
            barrier, inc=1, device_id={"rows": lax.rem(r + d, R)}, device_id_type=MESH
        )
    for d in range(1, Z):
        pl.semaphore_signal(
            barrier, inc=1, device_id={"rhs": lax.rem(z + d, Z)}, device_id_type=MESH
        )
    pl.semaphore_wait(barrier, R + Z - 2)

    copies = []
    for d in range(1, R):
        peer = lax.rem(r + d, R)
        copy = pltpu.make_async_remote_copy(
            src_ref=w_ref.at[peer],
            dst_ref=got.at[d],
            send_sem=send.at[d],
            recv_sem=recv.at[d],
            device_id={"rows": peer},
            device_id_type=MESH,
        )
        copy.start()
        copies.append(copy)
    total = w_ref[r]
    for d, copy in enumerate(copies, 1):
        copy.wait()
        total = total + got[d]
    out_ref[r, z] = total

    copies = []
    for d in range(1, Z):
        copy = pltpu.make_async_remote_copy(
            src_ref=out_ref.at[r, z],
            dst_ref=out_ref.at[r, z],
            send_sem=zsend.at[d],
            recv_sem=zrecv.at[d],
            device_id={"rhs": lax.rem(z + d, Z)},
            device_id_type=MESH,
        )
        copy.start()
        copies.append(copy)
    for copy in copies:
        copy.wait()

    half = R // 2
    spot = r // 2

    def to_sibling(i, where):
        copy = pltpu.make_async_remote_copy(
            src_ref=out_ref.at[where],
            dst_ref=out_ref.at[where],
            send_sem=csend.at[i],
            recv_sem=crecv.at[i],
            device_id={"rows": sibling},
            device_id_type=MESH,
        )
        copy.start()
        return copy

    across = []
    for d in range(1, half):
        copy = pltpu.make_async_remote_copy(
            src_ref=out_ref.at[r],
            dst_ref=out_ref.at[r],
            send_sem=psend.at[d],
            recv_sem=precv.at[d],
            device_id={"rows": lax.rem(spot + d, half) * 2 + core},
            device_id_type=MESH,
        )
        copy.start()
        across.append(copy)
    local = [to_sibling(0, r)]
    for d, copy in enumerate(across, 1):
        copy.wait()
        local.append(to_sibling(d, lax.rem(spot - d + half, half) * 2 + core))
    for copy in local:
        copy.wait()


def reduce_panels(w):
    R, Z = lax.axis_size("rows"), lax.axis_size("rhs")
    features, width = w.shape
    rows = features // R
    sems = pltpu.SemaphoreType.DMA
    return pl.pallas_call(
        functools.partial(reduce_kernel, R, Z),
        out_shape=jax.ShapeDtypeStruct((R, Z, rows, width), jnp.float32),
        in_specs=[VMEM],
        out_specs=VMEM,
        scratch_shapes=[pltpu.VMEM((R, rows, width), jnp.float32)]
        + [sems((R,))] * 2
        + [sems((Z,))] * 2
        + [sems((R,))] * 4,
        compiler_params=pltpu.CompilerParams(collective_id=1, has_side_effects=True),
    )(w.reshape(R, rows, width))


def invert_two(a, b, d):
    scale = 1.0 / (a * d - b * b)
    return d * scale, -b * scale, a * scale


def invert_four(p):
    e0, e1, e2 = invert_two(p[0][0], p[0][1], p[1][1])
    y00 = e0 * p[0][2] + e1 * p[1][2]
    y01 = e0 * p[0][3] + e1 * p[1][3]
    y10 = e1 * p[0][2] + e2 * p[1][2]
    y11 = e1 * p[0][3] + e2 * p[1][3]
    s0 = p[2][2] - (p[0][2] * y00 + p[1][2] * y10)
    s1 = p[2][3] - (p[0][2] * y01 + p[1][2] * y11)
    s2 = p[3][3] - (p[0][3] * y01 + p[1][3] * y11)
    t0, t1, t2 = invert_two(s0, s1, s2)
    q02 = -(y00 * t0 + y01 * t1)
    q03 = -(y00 * t1 + y01 * t2)
    q12 = -(y10 * t0 + y11 * t1)
    q13 = -(y10 * t1 + y11 * t2)
    q00 = e0 - (q02 * y00 + q03 * y01)
    q01 = e1 - (q02 * y10 + q03 * y11)
    q11 = e2 - (q12 * y10 + q13 * y11)
    return [
        [q00, q01, q02, q03],
        [q01, q11, q12, q13],
        [q02, q12, t0, t1],
        [q03, q13, t1, t2],
    ]


def invert_block(ref, dst):
    q = 4
    groups = TILE // 8
    a = [ref[8 * i : 8 * i + 8, :] for i in range(groups)]
    lane = lax.broadcasted_iota(jnp.int32, (8, TILE), 1)
    sub = lax.broadcasted_iota(jnp.int32, (8, TILE), 0)
    lane1 = lane[:1]
    for k in range(0, TILE, q):
        g, o = k // 8, k % 8
        c = [
            [jnp.broadcast_to(v[:, k + j : k + j + 1], (8, TILE)) for j in range(q)]
            for v in a
        ]
        p = [[c[g][j][o + i : o + i + 1, :] for j in range(q)] for i in range(q)]
        inv = invert_four(p)
        inside = jnp.logical_and(lane >= k, lane < k + q)
        pivot = [
            jnp.where(lane1 == k + i, 1.0, jnp.where(inside[:1], 0.0, a[g][o + i : o + i + 1, :]))
            for i in range(q)
        ]
        w = [sum(inv[i][j] * pivot[j] for j in range(q)) for i in range(q)]
        wb = [jnp.broadcast_to(v, (8, TILE)) for v in w]
        new = []
        for i in range(groups):
            v = jnp.where(inside, 0.0, a[i])
            v = v - ((c[i][0] * wb[0] + c[i][1] * wb[1]) + (c[i][2] * wb[2] + c[i][3] * wb[3]))
            if i == g:
                for j in range(q):
                    v = jnp.where(sub == o + j, wb[j], v)
            new.append(v)
        a = new
    for i in range(groups):
        dst[8 * i : 8 * i + 8, :] = a[i]


def solve_kernel(count, big_ref, coef_ref, low_ref, gram, right, inverse):
    R, Z, rows, width = big_ref.shape
    panel = width // 2
    size = gram.shape[0]
    for r in range(R):
        for z in range(Z):
            here = (slice(r * rows, (r + 1) * rows), slice(z * panel, (z + 1) * panel))
            gram[here] = big_ref[r, z, :, :panel] * (1.0 / count)
            right[here] = big_ref[r, z, :, panel:] * (1.0 / count)
    row = lax.broadcasted_iota(jnp.int32, (TILE, TILE), 0)
    col = lax.broadcasted_iota(jnp.int32, (TILE, TILE), 1)
    eye = jnp.where(row == col, jnp.float32(ridge), 0.0)
    blocks = size // TILE
    dot = functools.partial(jnp.dot, precision=HIGHEST, preferred_element_type=jnp.float32)

    def at(i):
        return slice(i * TILE, (i + 1) * TILE)

    for k in range(blocks):
        gram[at(k), at(k)] += eye
    tail = lambda k: slice((k + 1) * TILE, size)

    @pl.loop(0, blocks)
    def _(k):
        begin = pl.multiple_of(k * TILE, TILE)
        mine = pl.ds(begin, TILE)
        inverse[1] = gram[mine, mine]
        invert_block(inverse.at[1], inverse.at[0])
        inv = inverse[0]
        right[mine, :] = dot(inv, right[mine, :])
        gram_row = dot(inv, gram[mine, :])

        @pl.loop(k + 1, blocks)
        def _(i):
            below = pl.ds(pl.multiple_of(i * TILE, TILE), TILE)
            left = gram[below, mine]
            gram[below, :] -= dot(left, gram_row)
            right[below, :] -= dot(left, right[mine, :])

        gram[mine, :] = gram_row

    for k in reversed(range(blocks)):
        value = right[at(k), :]
        if k + 1 < blocks:
            value = value - dot(gram[at(k), tail(k)], right[tail(k), :])
            right[at(k), :] = value
        coef_ref[at(k), :] = value
        low_ref[at(k), :] = value.astype(jnp.bfloat16)


def solve(count, big):
    R, Z, rows, width = big.shape
    size, columns = R * rows, Z * width // 2
    return pl.pallas_call(
        functools.partial(solve_kernel, count),
        out_shape=[
            jax.ShapeDtypeStruct((size, columns), jnp.float32),
            jax.ShapeDtypeStruct((size, columns), jnp.bfloat16),
        ],
        in_specs=[VMEM],
        out_specs=[VMEM, VMEM],
        scratch_shapes=[
            pltpu.VMEM((size, size), jnp.float32),
            pltpu.VMEM((size, columns), jnp.float32),
            pltpu.VMEM((2, TILE, TILE), jnp.float32),
        ],
    )(big)


def body(samples, freq_table, feature_seeds, phases, treatment_features):
    count = samples.shape[0] * lax.axis_size("rows") * lax.axis_size("rhs")
    turn = jnp.float32(1.0 / (2.0 * math.pi))
    high, middle, low = split_low(freq_table[feature_seeds] * turn)
    shift = jnp.stack(split_low(phases * turn), axis=1)
    shift = jnp.pad(shift, ((0, 0), (0, high.shape[1] - shift.shape[1])))
    freqs = jnp.concatenate([high, middle, high, middle, low, high, shift], axis=1)
    gathered = gather_samples(samples.T)
    me = lax.axis_index("rhs").astype(jnp.int32).reshape(1)
    w, own = panels(me, gathered, freqs, treatment_features)
    coefficients, low_coef = solve(count, reduce_panels(w))
    fitted = lax.dot_general(
        own, low_coef, (((1,), (0,)), ((), ())), preferred_element_type=jnp.float32
    ).reshape(samples.shape[0], low_coef.shape[1])
    return (coefficients, fitted)


def solution(mesh):
    placed = (P(("rows", "rhs"), None), P(), P(), P(), P("rows", "rhs"))
    return jax.shard_map(
        body, mesh=mesh, in_specs=placed, out_specs=(P(), P(("rows", "rhs"), None)), check_vma=False
    )
```

time: 369 us -> 115 us (0.31); the launches traced: 365 us -> 115 us
  waiting for transfers between devices: 156 us -> 0 us
  other arithmetic: 122 us -> 1.47 us
  Pallas kernels: 0 us -> 104 us
  matrix products: 41.5 us -> 4.35 us
  local copies, waits for them, and re-layouts: 21.3 us -> 3.81 us
  between operations: 17.2 us -> 0.71 us
  starting transfers between devices: 6.53 us -> 0 us
    psum x1 -> x0, waiting for transfers between devices: 134 us -> none  [body(): cross = lax.psum(cross_part, ('rows', 'rhs')) / count]
    another operation x19 -> x1, other arithmetic: 119 us -> 0.02 us  [body(): shift = jnp.stack(split_low(phases * turn), axis=1)]
    pallas_call x0 -> x4, Pallas kernels: none -> 104 us  [the longest x1 35.6 us: reduce_panels(): pl.pallas_call(functools.partial(reduce_kernel, R, Z), out_shape=jax.Shap...]
    dot_general x4 -> x1, matrix products: 28 us -> 4.35 us  [body(): lax.dot_general(own, low_coef, (((1,), (0,)), ((), ())), preferred_elemen...]
    all_to_all x1 -> x0, waiting for transfers between devices: 22 us -> none  [body(): lax.all_to_all(treatment_features, 'rhs', split_axis=0, concat_axis=1, ti...]
    another operation x20 -> x0, matrix products: 13.5 us -> none  [the longest x6 5.92 us: body(): factor = jnp.linalg.cholesky(gram)]
    another operation x34 -> x4, local copies, waits for them, and re-layouts: 9.47 us -> 0.19 us  [body(): shift = jnp.stack(split_low(phases * turn), axis=1)]
    all_to_all x1 -> x0, starting transfers between devices: 6.49 us -> none  [body(): lax.all_to_all(treatment_features, 'rhs', split_axis=0, concat_axis=1, ti...]
  transfers between devices with their start and end apart: 2 -> 0, of which waited for: 2 -> 0; matrix products, arithmetic and copies ran while one was open for 7% -> 0% of each run, Pallas kernels for 0% -> 0%
where the time goes in v1:
time: 115 us
  Pallas kernels  104 us (90%)
  matrix products  4.35 us (4%)
  local copies, waits for them, and re-layouts  3.81 us (3%)
  other arithmetic  1.47 us (1%)
    pallas_call x1, Pallas kernels, reduce_panels(): pl.pallas_call(functools.partial(reduce_kernel, R, Z), out_shape=jax.Shap...  35.6 us
    pallas_call x1, Pallas kernels, solve(): pl.pallas_call(functools.partial(solve_kernel, count), out_shape=[jax.Sha...  31.8 us
    pallas_call x1, Pallas kernels, panels(): pl.pallas_call(panel_kernel, grid_spec=pltpu.PrefetchScalarGridSpec(num_s...  20.5 us
    pallas_call x1, Pallas kernels, gather_samples(): pl.pallas_call(functools.partial(gather_kernel, group), out_shape=jax.Sha...  16.3 us
    dot_general x1, matrix products, body(): lax.dot_general(own, low_coef, (((1,), (0,)), ((), ())), preferred_elemen...  4.35 us

profile of v1, /device:TPU:0, one launch (start us, length us, event | category | flops | bytes accessed | tf_op | source)
XLA Modules:
  0.0 114.5 jit_solution(6695918328767652957)
XLA Ops:
  0.6 0.7 compare_select_fusion
  1.3 0.7 reduce-precision_convert_fusion.3
  2.1 0.2 copy.19
  2.3 16.3 %shard_map.68.x_ref = f32[4,16,2048]{2,1,0:T(8,128)} custom-call(f32[16,2048]{1,0:T(8,128)} %bitcast.10), custom_call_target="tpu_custom_call" | custom-call | tf_op jit(solution)/shard_map/pallas_call | solution.py:57
  18.5 1.5 %copy.17 = f32[4096,16]{1,0:T(8,128)S(1)} copy(f32[4096,16]{0,1:T(8,128)} %param.6) | data formatting | bytes 524288 | tf_op args[1]
  20.1 1.0 gather_fusion
  21.1 0.1 fusion.2
  21.2 1.0 concatenate.3.f_ref
  22.2 20.5 %shard_map.69 = (f32[512,256]{1,0:T(8,128)}, bf16[2,512,1024]{2,1,0:T(8,128)(2,1)}) custom-call(s32[1]{0:T(128)} %bitcast.me_ref, f32[4,16,2048]{2,1,0:T(8,128)} %shard_map.68.x_ref, bf16[512,112]{1,0:T(8,128)(2,1)} %concatenate.3.f_ref, bf16[8192,128]{1,0:T(8,128)(2,1)} %t_ref.1), custom_call_target="tpu_custom_call" | custom-call | tf_op jit(solution)/shard_map/pallas_call | solution.py:111
  42.7 0.0 copy-start
  42.7 35.6 %shard_map.70.big_ref = f32[8,4,64,256]{3,2,1,0:T(8,128)} custom-call(f32[8,64,256]{2,1,0:T(8,128)} %bitcast.9), custom_call_target="tpu_custom_call" | custom-call | tf_op jit(solution)/shard_map/pallas_call | solution.py:223
  78.3 31.8 %shard_map.71 = (f32[512,512]{1,0:T(8,128)}, bf16[512,512]{1,0:T(8,128)(2,1)}) custom-call(f32[8,4,64,256]{3,2,1,0:T(8,128)} %shard_map.70.big_ref), custom_call_target="tpu_custom_call" | custom-call | tf_op jit(solution)/shard_map/pallas_call | solution.py:354
  110.2 0.0 copy-done
  110.2 4.3 %fusion = f32[2,1024,512]{2,1,0:T(8,128)} fusion(bf16[2,512,1024]{2,1,0:T(8,128)(2,1)S(1)} %copy-done, bf16[512,512]{1,0:T(8,128)(2,1)} %get-tuple-element.9), kind=kOutput, calls=%fused_computation.1 | convolution fusion | flops 1073741824 | bytes 6815744 | tf_op jit(solution)/shard_map/dot_general | solution.py:381
  (6 shorter events, 0.1 us)
Async XLA Ops:
  42.7 67.5 %copy-start = (bf16[2,512,1024]{2,1,0:T(8,128)(2,1)S(1)}, bf16[2,512,1024]{2,1,0:T(8,128)(2,1)}, u32[]{:S(2)}) copy-start(bf16[2,512,1024]{2,1,0:T(8,128)(2,1)} %get-tuple-element.8) | copy-start | bytes 6291460

commit v2 on v0

v2 whole, which is shorter than its diff:
```python
import functools
import math

import jax
import jax.numpy as jnp
from jax import lax
from jax.experimental import pallas as pl
from jax.experimental.pallas import tpu as pltpu
from jax.sharding import PartitionSpec as P

ridge = 0.05
MESH = pl.DeviceIdType.MESH
HIGHEST = lax.Precision.HIGHEST
VMEM = pl.BlockSpec(memory_space=pltpu.VMEM)
NT = (((1,), (1,)), ((), ()))
TILE = 128
SIN_TERMS = [3.1415926532437486, -5.167712741221454, 2.5501627947182053, -0.5992474048759052, 0.08203123002136099, -0.00700050017770637]


def split_low(x):
    high = lax.reduce_precision(x, 8, 7)
    rest = x - high
    middle = lax.reduce_precision(rest, 8, 7)
    low = rest - middle
    return tuple(t.astype(jnp.bfloat16) for t in (high, middle, low))


def feature_kernel(group, parts, x_ref, f_ref, t_hbm, gram_ref, cross_ref, own_ref, xs, t_ref, rhs, acc, *rest):
    phis, (send, recv, local) = rest[:parts], rest[parts:]
    me = lax.axis_index("rhs")
    own, panel = x_ref.shape[1], t_ref.shape[1]
    chunk = own // parts
    load = pltpu.make_async_copy(t_hbm, t_ref, local)
    load.start()
    barrier = pltpu.get_barrier_semaphore()
    for d in range(1, group):
        pl.semaphore_signal(
            barrier, inc=1, device_id={"rhs": lax.rem(me + d, group)}, device_id_type=MESH
        )
    pl.semaphore_wait(barrier, group - 1)

    def sending(d):
        return pltpu.make_async_remote_copy(
            src_ref=x_ref,
            dst_ref=xs.at[d],
            send_sem=send.at[d],
            recv_sem=recv.at[d],
            device_id={"rhs": lax.rem(me + d, group)},
            device_id_type=MESH,
        )

    for d in range(1, group):
        sending(d).start()
    xs[0] = x_ref[...]
    acc[...] = jnp.zeros_like(acc)
    load.wait()
    scale = math.sqrt(2.0 * math.sqrt(2.0))

    @pl.loop(0, group)
    def _(d):
        @pl.when(d > 0)
        def _():
            sending(d).wait()

        block = lax.rem(me - d + group, group)
        for part in range(parts):
            x = xs[d, :, part * chunk : (part + 1) * chunk]
            high = x.astype(jnp.bfloat16)
            left = x - high.astype(jnp.float32)
            middle = left.astype(jnp.bfloat16)
            low = (left - middle.astype(jnp.float32)).astype(jnp.bfloat16)
            ones = jnp.ones(x.shape, jnp.bfloat16)
            rows = jnp.concatenate([high, high, middle, middle, high, low, ones], axis=0)
            turns = jnp.dot(f_ref[...], rows, preferred_element_type=jnp.float32)
            r = turns - jnp.round(turns)
            u = r * r
            s = jnp.full_like(u, SIN_TERMS[-1] * scale)
            for term in reversed(SIN_TERMS[:-1]):
                s = s * u + term * scale
            s = s * r
            phis[part][...] = (math.sqrt(2.0) - s * s).astype(jnp.bfloat16)
            mine = phis[part][pl.ds(pl.multiple_of(me * panel, panel), panel), :]
            rhs[part, :, :panel] = mine.T
            here = pl.multiple_of(block * own + part * chunk, chunk)
            rhs[part, :, panel:] = t_ref[pl.ds(here, chunk), :]
            acc[...] += jnp.dot(phis[part][...], rhs[part], preferred_element_type=jnp.float32)

        @pl.when(d == 0)
        def _():
            for part in range(parts):
                own_ref[part] = phis[part][...]

    gram_ref[...] = acc[:, :panel]
    cross_ref[...] = acc[:, panel:]


def panels(x, freqs, targets):
    group = lax.axis_size("rhs")
    depth, own = x.shape
    features = freqs.shape[0]
    panel = targets.shape[1]
    chunk = min(own, 512)
    parts = own // chunk
    sems = pltpu.SemaphoreType.DMA
    return pl.pallas_call(
        functools.partial(feature_kernel, group, parts),
        in_specs=[VMEM, VMEM, pl.BlockSpec(memory_space=pl.ANY)],
        out_specs=[VMEM] * 3,
        out_shape=[
            jax.ShapeDtypeStruct((features, panel), jnp.float32),
            jax.ShapeDtypeStruct((features, panel), jnp.float32),
            jax.ShapeDtypeStruct((parts, features, chunk), jnp.bfloat16),
        ],
        scratch_shapes=[
            pltpu.VMEM((group, depth, own), jnp.float32),
            pltpu.VMEM(targets.shape, targets.dtype),
            pltpu.VMEM((parts, chunk, 2 * panel), jnp.bfloat16),
            pltpu.VMEM((features, 2 * panel), jnp.float32),
        ]
        + [pltpu.VMEM((features, chunk), jnp.bfloat16)] * parts
        + [sems((group,)), sems((group,)), sems(())],
        compiler_params=pltpu.CompilerParams(collective_id=0, has_side_effects=True),
    )(x, freqs, targets)


def exchange(R, Z, w_ref, got, out, sems):
    send, recv, zsend, zrecv, psend, precv, csend, crecv = sems
    r, z = lax.axis_index("rows"), lax.axis_index("rhs")
    core, spot, half = lax.rem(r, 2), r // 2, R // 2

    def copy(src, dst, out_sem, in_sem, d, peer):
        return pltpu.make_async_remote_copy(
            src_ref=src,
            dst_ref=dst,
            send_sem=out_sem.at[d],
            recv_sem=in_sem.at[d],
            device_id=peer,
            device_id_type=MESH,
        )

    def scatter(d):
        peer = lax.rem(r + d, R)
        return copy(w_ref.at[peer], got.at[d], send, recv, d, {"rows": peer})

    def along(d):
        mine = out.at[r, z]
        return copy(mine, mine, zsend, zrecv, d, {"rhs": lax.rem(z + d, Z)})

    def across(d):
        peer = lax.rem(spot + d, half) * 2 + core
        return copy(out.at[r], out.at[r], psend, precv, d, {"rows": peer})

    def aside(d):
        where = out.at[lax.rem(spot - d + half, half) * 2 + core]
        return copy(where, where, csend, crecv, d, {"rows": r + 1 - 2 * core})

    def first():
        for d in range(1, R):
            scatter(d).start()

    def second():
        total = w_ref[r]
        for d in range(1, R):
            scatter(d).wait()
            total = total + got[d]
        out[r, z] = total
        for d in range(1, Z):
            along(d).start()

    def third():
        for d in range(1, Z):
            along(d).wait()
        for d in range(1, half):
            across(d).start()
        aside(0).start()

    def fourth():
        for d in range(1, half):
            across(d).wait()
            aside(d).start()

    def last():
        for d in range(half):
            aside(d).wait()

    return first, second, third, fourth, last


def invert_two(a, b, d):
    scale = 1.0 / (a * d - b * b)
    return d * scale, -b * scale, a * scale


def invert_four(p):
    e0, e1, e2 = invert_two(p[0][0], p[0][1], p[1][1])
    y00 = e0 * p[0][2] + e1 * p[1][2]
    y01 = e0 * p[0][3] + e1 * p[1][3]
    y10 = e1 * p[0][2] + e2 * p[1][2]
    y11 = e1 * p[0][3] + e2 * p[1][3]
    s0 = p[2][2] - (p[0][2] * y00 + p[1][2] * y10)
    s1 = p[2][3] - (p[0][2] * y01 + p[1][2] * y11)
    s2 = p[3][3] - (p[0][3] * y01 + p[1][3] * y11)
    t0, t1, t2 = invert_two(s0, s1, s2)
    q02 = -(y00 * t0 + y01 * t1)
    q03 = -(y00 * t1 + y01 * t2)
    q12 = -(y10 * t0 + y11 * t1)
    q13 = -(y10 * t1 + y11 * t2)
    q00 = e0 - (q02 * y00 + q03 * y01)
    q01 = e1 - (q02 * y10 + q03 * y11)
    q11 = e2 - (q12 * y10 + q13 * y11)
    return [
        [q00, q01, q02, q03],
        [q01, q11, q12, q13],
        [q02, q12, t0, t1],
        [q03, q13, t1, t2],
    ]


def invert_block(ref, dst):
    q = 4
    groups = TILE // 8
    a = [ref[8 * i : 8 * i + 8, :] for i in range(groups)]
    lane = lax.broadcasted_iota(jnp.int32, (8, TILE), 1)
    sub = lax.broadcasted_iota(jnp.int32, (8, TILE), 0)
    lane1 = lane[:1]
    for k in range(0, TILE, q):
        g, o = k // 8, k % 8
        c = [
            [jnp.broadcast_to(v[:, k + j : k + j + 1], (8, TILE)) for j in range(q)]
            for v in a
        ]
        if k == 0:
            p = [[c[g][j][o + i : o + i + 1, :] for j in range(q)] for i in range(q)]
        inv = invert_four(p)
        n = k + q
        if n < TILE:
            after = [jnp.broadcast_to(a[g][:, n + j : n + j + 1], (8, TILE)) for j in range(q)]
            mine = [[v[o + i : o + i + 1, :] for v in after] for i in range(q)]
            if n // 8 != g:
                after = [
                    jnp.broadcast_to(a[n // 8][:, n + j : n + j + 1], (8, TILE)) for j in range(q)
                ]
            below = [[v[n % 8 + i : n % 8 + i + 1, :] for v in after] for i in range(q)]
            t = [[sum(inv[i][b] * mine[b][j] for b in range(q)) for j in range(q)] for i in range(q)]
            p = [
                [
                    below[i][j] - sum(mine[b][i] * t[b][j] for b in range(q)) if j >= i else None
                    for j in range(q)
                ]
                for i in range(q)
            ]
        inside = jnp.logical_and(lane >= k, lane < k + q)
        pivot = [
            jnp.where(lane1 == k + i, 1.0, jnp.where(inside[:1], 0.0, a[g][o + i : o + i + 1, :]))
            for i in range(q)
        ]
        w = [sum(inv[i][j] * pivot[j] for j in range(q)) for i in range(q)]
        wb = [jnp.broadcast_to(v, (8, TILE)) for v in w]
        new = []
        for i in range(groups):
            v = jnp.where(inside, 0.0, a[i])
            v = v - ((c[i][0] * wb[0] + c[i][1] * wb[1]) + (c[i][2] * wb[2] + c[i][3] * wb[3]))
            if i == g:
                for j in range(q):
                    v = jnp.where(sub == o + j, wb[j], v)
            new.append(v)
        a = new
    for i in range(groups):
        dst[8 * i : 8 * i + 8, :] = a[i]


def solve_kernel(R, Z, count, w_ref, v_ref, coef_ref, low_ref, gram, right, lower, inverse, got, out, vgot, vout, *sems):
    rows, panel = w_ref.shape[1:]
    size = gram.shape[0]
    r, z = lax.axis_index("rows"), lax.axis_index("rhs")
    barrier = pltpu.get_barrier_semaphore()
    for d in range(1, R):
        pl.semaphore_signal(
            barrier, inc=1, device_id={"rows": lax.rem(r + d, R)}, device_id_type=MESH
        )
    for d in range(1, Z):
        pl.semaphore_signal(
            barrier, inc=1, device_id={"rhs": lax.rem(z + d, Z)}, device_id_type=MESH
        )
    pl.semaphore_wait(barrier, R + Z - 2)
    for stage in exchange(R, Z, w_ref, got, out, sems[:8]):
        stage()
    stages = exchange(R, Z, v_ref, vgot, vout, sems[8:])
    stages[0]()

    def spread(source, dest):
        for i in range(R):
            for j in range(Z):
                dest[i * rows : (i + 1) * rows, j * panel : (j + 1) * panel] = source[
                    i, j
                ] * (1.0 / count)

    spread(out, gram)
    row = lax.broadcasted_iota(jnp.int32, (TILE, TILE), 0)
    col = lax.broadcasted_iota(jnp.int32, (TILE, TILE), 1)
    eye = jnp.where(row == col, jnp.float32(ridge), 0.0)
    blocks = size // TILE
    dot = functools.partial(jnp.dot, precision=HIGHEST, preferred_element_type=jnp.float32)

    def at(i):
        return slice(i * TILE, (i + 1) * TILE)

    for k in range(blocks):
        gram[at(k), at(k)] += eye

    @pl.loop(0, blocks)
    def _(k):
        mine = pl.ds(pl.multiple_of(k * TILE, TILE), TILE)
        inverse[blocks] = gram[mine, mine]
        invert_block(inverse.at[blocks], inverse.at[k])
        gram_row = dot(inverse[k], gram[mine, :])

        @pl.loop(k + 1, blocks)
        def _(i):
            below = pl.ds(pl.multiple_of(i * TILE, TILE), TILE)
            left = gram[below, mine]
            lower[below, mine] = left
            gram[below, :] -= dot(left, gram_row)

        gram[mine, :] = gram_row
        for i, stage in enumerate(stages[1:]):
            pl.when(k == min(i, blocks - 1))(stage)

    spread(vout, right)
    for k in range(blocks):
        value = dot(inverse[k], right[at(k), :])
        right[at(k), :] = value
        if k + 1 < blocks:
            tail = slice((k + 1) * TILE, size)
            right[tail, :] -= dot(lower[tail, at(k)], value)
    for k in reversed(range(blocks)):
        value = right[at(k), :]
        coef_ref[at(k), :] = value
        low_ref[at(k), :] = value.astype(jnp.bfloat16)
        if k:
            right[: k * TILE, :] -= dot(gram[: k * TILE, at(k)], value)


def solve(count, w, v):
    R, Z = lax.axis_size("rows"), lax.axis_size("rhs")
    size, panel = w.shape
    rows, columns = size // R, Z * panel
    split = (R, rows, panel)
    sems = pltpu.SemaphoreType.DMA
    blocks = size // TILE
    big = pltpu.VMEM((R, Z, rows, panel), jnp.float32)
    return pl.pallas_call(
        functools.partial(solve_kernel, R, Z, count),
        out_shape=[
            jax.ShapeDtypeStruct((size, columns), jnp.float32),
            jax.ShapeDtypeStruct((size, columns), jnp.bfloat16),
        ],
        in_specs=[VMEM, VMEM],
        out_specs=[VMEM, VMEM],
        scratch_shapes=[
            pltpu.VMEM((size, size), jnp.float32),
            pltpu.VMEM((size, columns), jnp.float32),
            pltpu.VMEM((size, size), jnp.float32),
            pltpu.VMEM((blocks + 1, TILE, TILE), jnp.float32),
            pltpu.VMEM(split, jnp.float32),
            big,
            pltpu.VMEM(split, jnp.float32),
            big,
        ]
        + ([sems((R,))] * 2 + [sems((Z,))] * 2 + [sems((R,))] * 4) * 2,
        compiler_params=pltpu.CompilerParams(collective_id=1, has_side_effects=True),
    )(w.reshape(split), v.reshape(split))


def body(samples, freq_table, feature_seeds, phases, treatment_features):
    count = samples.shape[0] * lax.axis_size("rows") * lax.axis_size("rhs")
    turn = jnp.float32(1.0 / (2.0 * math.pi))
    high, middle, low = split_low(freq_table[feature_seeds] * turn)
    shift = jnp.stack(split_low(phases * turn), axis=1)
    shift = jnp.pad(shift, ((0, 0), (0, high.shape[1] - shift.shape[1])))
    freqs = jnp.concatenate([high, middle, high, middle, low, high, shift], axis=1)
    w, v, own = panels(samples.T, freqs, treatment_features)
    coefficients, low_coef = solve(count, w, v)
    fitted = lax.dot_general(
        own, low_coef, (((1,), (0,)), ((), ())), preferred_element_type=jnp.float32
    ).reshape(samples.shape[0], low_coef.shape[1])
    return (coefficients, fitted)


def solution(mesh):
    placed = (P(("rows", "rhs"), None), P(), P(), P(), P("rows", "rhs"))
    return jax.shard_map(
        body, mesh=mesh, in_specs=placed, out_specs=(P(), P(("rows", "rhs"), None)), check_vma=False
    )
```

time: 369 us -> 93.9 us (0.25); the launches traced: 365 us -> 93.7 us
  waiting for transfers between devices: 156 us -> 0 us
  other arithmetic: 122 us -> 1.47 us
  Pallas kernels: 0 us -> 81.6 us
  matrix products: 41.5 us -> 5.06 us
  local copies, waits for them, and re-layouts: 21.3 us -> 4.78 us
  between operations: 17.2 us -> 0.71 us
  starting transfers between devices: 6.53 us -> 0 us
    psum x1 -> x0, waiting for transfers between devices: 134 us -> none  [body(): cross = lax.psum(cross_part, ('rows', 'rhs')) / count]
    another operation x19 -> x1, other arithmetic: 119 us -> 0.02 us  [body(): shift = jnp.stack(split_low(phases * turn), axis=1)]
    pallas_call x0 -> x2, Pallas kernels: none -> 81.6 us  [the longest x1 58.3 us: solve(): pl.pallas_call(functools.partial(solve_kernel, R, Z, count), out_shape=[j...]
    dot_general x4 -> x1, matrix products: 28 us -> 5.06 us  [body(): lax.dot_general(own, low_coef, (((1,), (0,)), ((), ())), preferred_elemen...]
    all_to_all x1 -> x0, waiting for transfers between devices: 22 us -> none  [body(): lax.all_to_all(treatment_features, 'rhs', split_axis=0, concat_axis=1, ti...]
    another operation x20 -> x0, matrix products: 13.5 us -> none  [the longest x6 5.92 us: body(): factor = jnp.linalg.cholesky(gram)]
    another operation x34 -> x4, local copies, waits for them, and re-layouts: 9.47 us -> 0.19 us  [body(): shift = jnp.stack(split_low(phases * turn), axis=1)]
    all_to_all x1 -> x0, starting transfers between devices: 6.49 us -> none  [body(): lax.all_to_all(treatment_features, 'rhs', split_axis=0, concat_axis=1, ti...]
  transfers between devices with their start and end apart: 2 -> 0, of which waited for: 2 -> 0; matrix products, arithmetic and copies ran while one was open for 7% -> 0% of each run, Pallas kernels for 0% -> 0%
where the time goes in v2:
time: 93.9 us; the launch traced here: 93.7 us
  Pallas kernels  81.6 us (87%)
  matrix products  5.06 us (5%)
  local copies, waits for them, and re-layouts  4.78 us (5%)
  other arithmetic  1.47 us (2%)
    pallas_call x1, Pallas kernels, solve(): pl.pallas_call(functools.partial(solve_kernel, R, Z, count), out_shape=[j...  58.3 us
    pallas_call x1, Pallas kernels, panels(): pl.pallas_call(functools.partial(feature_kernel, group, parts), in_specs=...  23.3 us
    dot_general x1, matrix products, body(): lax.dot_general(own, low_coef, (((1,), (0,)), ((), ())), preferred_elemen...  5.06 us
    unnamed x4, local copies, waits for them, and re-layouts  2.52 us

profile of v2, /device:TPU:0, one launch (start us, length us, event | category | flops | bytes accessed | tf_op | source)
XLA Modules:
  0.0 93.7 jit_solution(16055437379036999334)
XLA Ops:
  0.6 0.7 compare_select_fusion
  1.3 0.7 reduce-precision_convert_fusion.3
  2.1 0.2 copy.19
  2.3 1.5 %copy.17 = f32[4096,16]{1,0:T(8,128)S(1)} copy(f32[4096,16]{0,1:T(8,128)} %param.6) | data formatting | bytes 524288 | tf_op args[1]
  3.8 1.0 %gather_fusion = f32[512,16]{1,0:T(8,128)S(1)} fusion(f32[4096,16]{1,0:T(8,128)S(1)} %copy.17, s32[1024]{0:T(1024)S(1)} %pad_clamp_fusion), kind=kCustom, calls=%fused_computation | custom fusion | bytes 67584 | tf_op jit(solution)/shard_map/gather | solution.py:378
  4.9 0.1 fusion.2
  5.0 1.0 %concatenate.3.f_ref = bf16[512,112]{1,0:T(8,128)(2,1)} concatenate(bf16[512,16]{1,0:T(8,128)(2,1)S(1)} %get-tuple-element.14, bf16[512,16]{1,0:T(8,128)(2,1)S(1)} %get-tuple-element.13, bf16[512,16]{1,0:T(8,128)(2,1)S(1)} %get-tuple-element.14, bf16[512,16]{1,0:T(8,128)(2,1)S(1)} %get-tuple-element.13, bf16[512,16]{1,0:T(8,128)(2,1)S(1)} %get-tuple-element.12, ...), dimensions={1} | concatenate | bytes 229376 | tf_op jit(solution)/shard_map/concatenate | solution.py:381
  6.0 23.3 %shard_map.68 = (f32[512,128]{1,0:T(8,128)}, f32[512,128]{1,0:T(8,128)}, bf16[4,512,512]{2,1,0:T(8,128)(2,1)}) custom-call(f32[16,2048]{1,0:T(8,128)} %bitcast.11, bf16[512,112]{1,0:T(8,128)(2,1)} %concatenate.3.f_ref, bf16[8192,128]{1,0:T(8,128)(2,1)} %t_hbm.1), custom_call_target="tpu_custom_call" | custom-call | tf_op jit(solution)/shard_map/pallas_call | solution.py:105
  29.3 58.3 %shard_map.69 = (f32[512,512]{1,0:T(8,128)}, bf16[512,512]{1,0:T(8,128)(2,1)}) custom-call(f32[8,64,128]{2,1,0:T(8,128)} %bitcast.9, f32[8,64,128]{2,1,0:T(8,128)} %bitcast.10), custom_call_target="tpu_custom_call" | custom-call | tf_op jit(solution)/shard_map/pallas_call | solution.py:352
  87.6 0.0 copy-start
  87.6 5.1 %fusion = f32[4,512,512]{2,1,0:T(8,128)} fusion(bf16[4,512,512]{2,1,0:T(8,128)(2,1)} %get-tuple-element.10, bf16[512,512]{1,0:T(8,128)(2,1)} %get-tuple-element.11), kind=kOutput, calls=%fused_computation.1 | convolution fusion | flops 1073741824 | bytes 6815744 | tf_op jit(solution)/shard_map/dot_general | solution.py:384
  92.7 0.0 copy-done
  92.7 1.0 %copy.23 = f32[512,512]{1,0:T(8,128)} copy(f32[512,512]{1,0:T(8,128)S(1)} %copy-done) | data formatting | bytes 2097152
  (6 shorter events, 0.1 us)
Async XLA Ops:
  87.6 5.1 %copy-start = (f32[512,512]{1,0:T(8,128)S(1)}, f32[512,512]{1,0:T(8,128)}, u32[]{:S(2)}) copy-start(f32[512,512]{1,0:T(8,128)} %get-tuple-element.20) | copy-start | bytes 3145732

commit v3 on v2

--- a/solution.py
+++ b/solution.py
@@ -39,32 +39,60 @@
         )
     pl.semaphore_wait(barrier, group - 1)
 
-    def sending(d):
+    def moving(d, way):
+        block = me - way * (d - 1)
         return pltpu.make_async_remote_copy(
-            src_ref=x_ref,
-            dst_ref=xs.at[d],
-            send_sem=send.at[d],
-            recv_sem=recv.at[d],
-            device_id={"rhs": lax.rem(me + d, group)},
+            src_ref=x_ref if isinstance(d, int) and d == 1 else xs.at[block],
+            dst_ref=xs.at[block],
+            send_sem=send.at[(way + 1) // 2, d],
+            recv_sem=recv.at[(way + 1) // 2, d],
+            device_id={"rhs": me + way},
             device_id_type=MESH,
         )
 
-    for d in range(1, group):
-        sending(d).start()
-    xs[0] = x_ref[...]
+    def arriving(d, way):
+        block = me - way * d
+        return pltpu.make_async_remote_copy(
+            src_ref=xs.at[block],
+            dst_ref=xs.at[block],
+            send_sem=send.at[(way + 1) // 2, d],
+            recv_sem=recv.at[(way + 1) // 2, d],
+            device_id={"rhs": me - way},
+            device_id_type=MESH,
+        )
+
+    def inside(v):
+        return jnp.logical_and(v >= 0, v < group)
+
+    def pass_on(d, way):
+        pl.when(jnp.logical_and(inside(me + way), inside(me - way * (d - 1))))(
+            lambda: moving(d, way).start()
+        )
+
+    xs[me] = x_ref[...]
+    for way in (1, -1):
+        pass_on(1, way)
     acc[...] = jnp.zeros_like(acc)
     load.wait()
+    near = jnp.minimum(me, group - 1 - me)
     scale = math.sqrt(2.0 * math.sqrt(2.0))
 
     @pl.loop(0, group)
     def _(d):
-        @pl.when(d > 0)
-        def _():
-            sending(d).wait()
-
-        block = lax.rem(me - d + group, group)
+        for way in (1, -1):
+
+            @pl.when(jnp.logical_and(d > 0, inside(me - way * d)))
+            def _():
+                arriving(d, way).wait_recv()
+
+            pl.when(jnp.logical_and(d > 0, d + 1 < group))(lambda: pass_on(d + 1, way))
+
+        step = (d + 1) // 2
+        both = jnp.where(d % 2 == 1, me - step, me + step)
+        single = jnp.where(me < group - 1 - me, me + d - near, me - d + near)
+        block = jnp.where(d <= 2 * near, both, single)
         for part in range(parts):
-            x = xs[d, :, part * chunk : (part + 1) * chunk]
+            x = xs[block, :, part * chunk : (part + 1) * chunk]
             high = x.astype(jnp.bfloat16)
             left = x - high.astype(jnp.float32)
             middle = left.astype(jnp.bfloat16)
@@ -90,6 +118,11 @@
             for part in range(parts):
                 own_ref[part] = phis[part][...]
 
+    for d in range(1, group):
+        for way in (1, -1):
+            pl.when(jnp.logical_and(inside(me + way), inside(me - way * (d - 1))))(
+                lambda: moving(d, way).wait_send()
+            )
     gram_ref[...] = acc[:, :panel]
     cross_ref[...] = acc[:, panel:]
 
@@ -118,7 +151,7 @@
             pltpu.VMEM((features, 2 * panel), jnp.float32),
         ]
         + [pltpu.VMEM((features, chunk), jnp.bfloat16)] * parts
-        + [sems((group,)), sems((group,)), sems(())],
+        + [sems((2, group)), sems((2, group)), sems(())],
         compiler_params=pltpu.CompilerParams(collective_id=0, has_side_effects=True),
     )(x, freqs, targets)
 

time: 93.9 us -> 88.7 us (0.945)
  Pallas kernels: 81.6 us -> 76.4 us
    pallas_call x1, Pallas kernels: 58.3 us -> 53.9 us  [solve(): pl.pallas_call(functools.partial(solve_kernel, R, Z, count), out_shape=[j...]
where the time goes in v3:
time: 88.7 us; the launch traced here: 88.4 us
  Pallas kernels  76.4 us (86%)
  matrix products  5.06 us (6%)
  local copies, waits for them, and re-layouts  4.78 us (5%)
  other arithmetic  1.47 us (2%)
    pallas_call x1, Pallas kernels, solve(): pl.pallas_call(functools.partial(solve_kernel, R, Z, count), out_shape=[j...  53.9 us
    pallas_call x1, Pallas kernels, panels(): pl.pallas_call(functools.partial(feature_kernel, group, parts), in_specs=...  22.5 us
    dot_general x1, matrix products, body(): lax.dot_general(own, low_coef, (((1,), (0,)), ((), ())), preferred_elemen...  5.06 us
    unnamed x4, local copies, waits for them, and re-layouts  2.52 us

profile of v3, /device:TPU:0, one launch (start us, length us, event | category | flops | bytes accessed | tf_op | source)
XLA Modules:
  0.0 88.4 jit_solution(7166289175293367048)
XLA Ops:
  0.6 0.7 compare_select_fusion
  1.3 0.7 reduce-precision_convert_fusion.3
  2.1 0.2 copy.19
  2.3 1.5 %copy.17 = f32[4096,16]{1,0:T(8,128)S(1)} copy(f32[4096,16]{0,1:T(8,128)} %param.6) | data formatting | bytes 524288 | tf_op args[1]
  3.8 1.0 %gather_fusion = f32[512,16]{1,0:T(8,128)S(1)} fusion(f32[4096,16]{1,0:T(8,128)S(1)} %copy.17, s32[1024]{0:T(1024)S(1)} %pad_clamp_fusion), kind=kCustom, calls=%fused_computation | custom fusion | bytes 67584 | tf_op jit(solution)/shard_map/gather | solution.py:411
  4.9 0.1 fusion.2
  5.0 1.0 %concatenate.3.f_ref = bf16[512,112]{1,0:T(8,128)(2,1)} concatenate(bf16[512,16]{1,0:T(8,128)(2,1)S(1)} %get-tuple-element.14, bf16[512,16]{1,0:T(8,128)(2,1)S(1)} %get-tuple-element.13, bf16[512,16]{1,0:T(8,128)(2,1)S(1)} %get-tuple-element.14, bf16[512,16]{1,0:T(8,128)(2,1)S(1)} %get-tuple-element.13, bf16[512,16]{1,0:T(8,128)(2,1)S(1)} %get-tuple-element.12, ...), dimensions={1} | concatenate | bytes 229376 | tf_op jit(solution)/shard_map/concatenate | solution.py:414
  6.0 22.5 %shard_map.68 = (f32[512,128]{1,0:T(8,128)}, f32[512,128]{1,0:T(8,128)}, bf16[4,512,512]{2,1,0:T(8,128)(2,1)}) custom-call(f32[16,2048]{1,0:T(8,128)} %bitcast.11, bf16[512,112]{1,0:T(8,128)(2,1)} %concatenate.3.f_ref, bf16[8192,128]{1,0:T(8,128)(2,1)} %t_hbm.1), custom_call_target="tpu_custom_call" | custom-call | tf_op jit(solution)/shard_map/pallas_call | solution.py:138
  28.5 53.9 %shard_map.69 = (f32[512,512]{1,0:T(8,128)}, bf16[512,512]{1,0:T(8,128)(2,1)}) custom-call(f32[8,64,128]{2,1,0:T(8,128)} %bitcast.9, f32[8,64,128]{2,1,0:T(8,128)} %bitcast.10), custom_call_target="tpu_custom_call" | custom-call | tf_op jit(solution)/shard_map/pallas_call | solution.py:385
  82.4 0.0 copy-start
  82.4 5.1 %fusion = f32[4,512,512]{2,1,0:T(8,128)} fusion(bf16[4,512,512]{2,1,0:T(8,128)(2,1)} %get-tuple-element.10, bf16[512,512]{1,0:T(8,128)(2,1)} %get-tuple-element.11), kind=kOutput, calls=%fused_computation.1 | convolution fusion | flops 1073741824 | bytes 6815744 | tf_op jit(solution)/shard_map/dot_general | solution.py:417
  87.5 0.0 copy-done
  87.5 1.0 %copy.23 = f32[512,512]{1,0:T(8,128)} copy(f32[512,512]{1,0:T(8,128)S(1)} %copy-done) | data formatting | bytes 2097152
  (6 shorter events, 0.1 us)
Async XLA Ops:
  82.4 5.1 %copy-start = (f32[512,512]{1,0:T(8,128)S(1)}, f32[512,512]{1,0:T(8,128)}, u32[]{:S(2)}) copy-start(f32[512,512]{1,0:T(8,128)} %get-tuple-element.20) | copy-start | bytes 3145732
